TPU v7x, 32 devices: a whole 2x2x4 slice. The times are simulated.
32 devices in a mesh: tm: 2 (over core), tile: 16 (over z, y, x).
Axes of the slice: x: 2, y: 2, z: 4, core: 2. Of those that a mesh axis runs over, the one named last changes fastest.
Arguments:
- features: bfloat16 [1, 8, 64, 64, 192], P(None, 'tm', 'tile'), may hold values from -60 to 60
- gain_one: float32 [192], replicated, may hold values from 0.5 to 1.5
- shift_one: float32 [192], replicated, may hold values from -3 to 3
- kernel_one: bfloat16 [3, 3, 3, 192, 192], replicated, may hold values from -0.078125 to 0.078125
- bias_one: float32 [192], replicated, may hold values from -3 to 3
- gain_two: float32 [192], replicated, may hold values from 0.5 to 1.5
- shift_two: float32 [192], replicated, may hold values from -3 to 3
- kernel_two: bfloat16 [3, 3, 3, 192, 192], replicated, may hold values from -0.078125 to 0.078125
- bias_two: float32 [192], replicated, may hold values from -3 to 3
- up_kernel: bfloat16 [3, 3, 192, 96], replicated, may hold values from -0.15625 to 0.15625
- up_bias: float32 [96], replicated, may hold values from -3 to 3
Outputs:
- decoded: bfloat16 [1, 8, 128, 64, 192], P(None, 'tm', 'tile')
All inputs are finite; a program needn't handle non-finite values.
Results may differ from a plain program's by a relative error of at most 0.009.
Values may be sent and summed in bfloat16 or wider, within the bound.
A program may use at most 128 MiB of HBM per device.

v0:
```python
import functools

import jax
import jax.numpy as jnp
from jax import lax
from jax.experimental import pallas as pl
from jax.experimental.pallas import tpu as pltpu
from jax.sharding import PartitionSpec as P

MESH = pl.DeviceIdType.MESH
G = 32
EPS = 1e-06
KP = 640
ORDER = (2, 3, 0, 1)


def split_dot(value, picks):
    m = value.shape[0]
    high = value.astype(jnp.bfloat16).astype(jnp.float32)
    rest = value - high
    mid = rest.astype(jnp.bfloat16).astype(jnp.float32)
    low = rest - mid
    terms = jnp.concatenate([high, mid, low], axis=0).astype(jnp.bfloat16)
    made = jnp.dot(terms, picks, preferred_element_type=jnp.float32)
    return made[0:m] + made[m:2 * m] + made[2 * m:3 * m]


def kernel(
    n,
    feat, g1_h, s1_h, k1, b1_h, g2_h, s2_h, k2, b2_h, uk, ub_h,
    out,
    x_ext, h_ext, j_ext, act, jact, w1, w2, wup, ukv, vecs, ubv, norm, gmap, smap, st_own, st_prev, st_fwd, beside,
    loc_sem, bulk_send, bulk_recv, own_send, own_recv, prev_send, prev_recv,
):
    frames, rows, cols, chans = feat.shape
    bf16, f32 = jnp.bfloat16, jnp.float32
    tm = lax.axis_index("tm")
    tile = lax.axis_index("tile")
    up_ok = tile > 0
    down_ok = tile < n - 1
    first = tm == 0
    later = tm > 0
    above = lax.rem(tile + n - 1, n)
    below = lax.rem(tile + 1, n)
    per = chans // G
    half = chans // 2
    inverse = 1.0 / float(n * rows * cols * per)
    old = frames - 2

    def local(i, s, d):
        copy = pltpu.make_async_copy(s, d, loc_sem.at[i])
        copy.start()
        return copy

    load_x = local(0, feat, x_ext.at[pl.ds(2, frames), pl.ds(1, rows)])

    barrier = pltpu.get_barrier_semaphore()
    for d in range(1, n):
        to = lax.rem(tile + d, n)
        pl.semaphore_signal(barrier, inc=1, device_id=(tm, to), device_id_type=MESH)
    for to in (tile, above, below):
        pl.semaphore_signal(barrier, inc=1, device_id=(1 - tm, to), device_id_type=MESH)

    load_u = local(1, uk, ukv)
    load_v = [
        local(4 + i, ref, vecs.at[i])
        for i, ref in enumerate((g1_h, s1_h, b1_h, g2_h, s2_h, b2_h))
    ]
    load_b = local(10, ub_h, ubv)
    load_1 = local(2, k1, w1.at[:, pl.ds(0, 3 * chans)])
    load_2 = local(3, k2, w2.at[:, pl.ds(0, 3 * chans)])

    def remote(slot, i, s, d, who):
        return pltpu.make_async_remote_copy(
            src_ref=s, dst_ref=d,
            send_sem=bulk_send.at[slot, i], recv_sem=bulk_recv.at[slot, i],
            device_id=who, device_id_type=MESH,
        )

    pending = []

    def start_all(copies):
        for copy, sends, _ in copies:
            pl.when(sends)(copy.start)
        pending.extend(copies)

    def wait_all(copies):
        for copy, _, gets in copies:
            pl.when(gets)(copy.wait_recv)

    def same_rows(slot, src, row0, f0, count, dst, g0):
        f, g = pl.ds(f0, count), pl.ds(g0, count)
        return [
            (remote(slot, 0, src.at[f, row0 + rows - 1], dst.at[g, 0], (tm, below)), down_ok, up_ok),
            (remote(slot, 1, src.at[f, row0], dst.at[g, rows + 1], (tm, above)), up_ok, down_ok),
        ]

    def next_frames(slot, src, row0, f0, count, dst, g0):
        f, g = pl.ds(f0, count), pl.ds(g0, count)
        return [
            (remote(slot, 2, src.at[f, pl.ds(row0, rows)], dst.at[g, pl.ds(1, rows)], (1, tile)), first, later),
            (remote(slot, 3, src.at[f, row0 + rows - 1], dst.at[g, 0], (1, below)), first & down_ok, later & up_ok),
            (remote(slot, 4, src.at[f, row0], dst.at[g, rows + 1], (1, above)), first & up_ok, later & down_ok),
        ]

    sent = []

    def own_copy(slot, d):
        return pltpu.make_async_remote_copy(
            src_ref=st_own.at[slot, 0, pl.ds(0, 2)], dst_ref=st_own.at[slot, d, pl.ds(0, 2)],
            send_sem=own_send.at[slot], recv_sem=own_recv.at[slot],
            device_id=(tm, lax.rem(tile + d, n)), device_id_type=MESH)

    def forward(slot):
        return pltpu.make_async_remote_copy(
            src_ref=st_fwd.at[slot, pl.ds(0, 2)], dst_ref=st_prev.at[slot, pl.ds(0, 2)],
            send_sem=prev_send.at[slot], recv_sem=prev_recv.at[slot],
            device_id=(1, tile), device_id_type=MESH)

    def send_total(slot, total):
        st_fwd[slot, 0:2] = total
        pl.when(first)(forward(slot).start)

    def own_all(slot):
        view = st_own.at[slot, pl.ds(1, n - 1), pl.ds(0, 2)]
        return pltpu.make_async_remote_copy(
            src_ref=view, dst_ref=view, send_sem=own_send.at[slot], recv_sem=own_recv.at[slot],
            device_id=(tm, below), device_id_type=MESH)

    def send_sums(slot, message):
        st_own[slot, 0, 0:2] = message
        for d in range(1, n):
            own_copy(slot, d).start()
        sent.append(slot)

    def sums_of(flat):
        return jnp.concatenate(
            [jnp.sum(flat, axis=0, keepdims=True), jnp.sum(flat * flat, axis=0, keepdims=True)], axis=0
        )

    def norm_from(slot, total, f, gain):
        both = split_dot(total, smap[f]) * inverse
        mean = both[0:1]
        var = both[1:2] - mean * mean
        norm[slot, 0:1] = mean
        norm[slot, 1:2] = 0.5 * (lax.rsqrt(var + EPS) * gain)

    def own_total(slot):
        return jnp.sum(st_own[slot], axis=0)[0:2]

    def prev_total(slot):
        return st_prev[slot, 0:2]

    beside[:, 0:8] = jnp.zeros((rows + 2, 8, chans), f32)
    beside[:, 8 + cols:16 + cols] = jnp.zeros((rows + 2, 8, chans), f32)

    def put_shifted(dst, f, r, value):
        beside[r, 8:8 + cols] = value
        left = beside[r, 7:7 + cols]
        right = beside[r, 9:9 + cols]
        dst[f, r, :, 0:chans] = left.astype(bf16)
        dst[f, r, :, chans:2 * chans] = value.astype(bf16)
        dst[f, r, :, 2 * chans:3 * chans] = right.astype(bf16)

    def act_frame(src, f, shift):
        mean, scale = norm[f, 0:1], norm[f, 1:2]
        for r in range(rows + 2):
            part = (src[f, r].astype(f32) - mean) * scale + shift
            value = part + part * jnp.tanh(part)
            ok = up_ok if r == 0 else down_ok if r == rows + 1 else None
            if f < 2:
                ok = later if ok is None else ok & later
            if ok is not None:
                value = jnp.where(ok, value, 0.0)
            put_shifted(act, f, r, value)

    def conv(f, w):
        parts = [
            act[f + i, j:j + rows].reshape(rows * cols, KP) for i in range(3) for j in range(3)
        ]
        return jnp.dot(
            jnp.concatenate(parts, axis=-1), w[...].reshape(9 * KP, chans), preferred_element_type=f32
        )

    lane = lax.broadcasted_iota(jnp.int32, (chans, 128), 1)
    chan = lax.broadcasted_iota(jnp.int32, (chans, 128), 0)
    lane_t = lax.broadcasted_iota(jnp.int32, (128, chans), 0)
    chan_t = lax.broadcasted_iota(jnp.int32, (128, chans), 1)
    for f in range(frames):
        low = (lane - f * G) * per
        gmap[f] = jnp.where((chan >= low) & (chan < low + per), 1.0, 0.0).astype(bf16)
        low = (lane_t - f * G) * per
        smap[f] = jnp.where((chan_t >= low) & (chan_t < low + per), 1.0, 0.0).astype(bf16)

    load_x.wait()
    message = jnp.zeros((2, 128), f32)
    for f in range(frames):
        flat = x_ext[2 + f, 1:1 + rows].reshape(rows * cols, chans).astype(f32)
        message = message + split_dot(sums_of(flat), gmap[f])

    own_one = same_rows(0, feat, 0, 0, frames, x_ext, 2)
    prev_one = next_frames(0, feat, 0, old, 2, x_ext, 0)
    pl.semaphore_wait(barrier, n + 2)
    send_sums(0, message)
    start_all(own_one + prev_one)

    pad = KP - 3 * chans
    act[:, :, :, 3 * chans:KP] = jnp.zeros((frames + 2, rows + 2, cols, pad), bf16)
    jact[:, :, :, 3 * chans:KP] = jnp.zeros((frames, rows + 2, cols, pad), bf16)
    w1[:, 3 * chans:KP] = jnp.zeros((9, pad, chans), bf16)
    w2[:, 3 * chans:KP] = jnp.zeros((9, pad, chans), bf16)
    wup[:, :, 3 * chans:KP] = jnp.zeros((2, 2, pad, chans), bf16)
    load_u.wait()
    for r in range(2):
        for dy in range(2):
            js = (((0,), (1, 2)) if r == 0 else ((0, 1), (2,)))[dy]
            line = [
                functools.reduce(jnp.add, [ukv[j, k].astype(f32) for j in js]) for k in range(3)
            ]
            zero = jnp.zeros_like(line[0])
            pieces = [(line[0], zero), (line[1] + line[2], line[0] + line[1]), (zero, line[2])]
            for dx, (even, odd) in enumerate(pieces):
                wup[r, dy, dx * chans:(dx + 1) * chans, 0:half] = even.astype(bf16)
                wup[r, dy, dx * chans:(dx + 1) * chans, half:chans] = odd.astype(bf16)
    for copy in load_v:
        copy.wait()
    load_b.wait()
    vecs[6, :, 0:half] = ubv[...]
    vecs[6, :, half:chans] = ubv[...]
    load_1.wait()

    own_all(0).wait_recv()
    wait_all(own_one)
    gain, shift = vecs[0], 0.5 * vecs[1]
    total = own_total(0)
    send_total(0, total)
    for f in range(frames):
        norm_from(2 + f, total, f, gain)

    halos = {}

    def hidden_frame(f):
        hidden = (conv(f, w1) + vecs[2]).astype(bf16)
        h_ext[2 + f, 1:1 + rows] = hidden.reshape(rows, cols, chans)
        return split_dot(sums_of(hidden.astype(f32)), gmap[0])

    def hidden_send(f, message):
        send_sums(1 + f, message)
        halos[f] = same_rows(1 + f, h_ext, 1, 2 + f, 1, h_ext, 2 + f)
        ahead = []
        if f >= old:
            ahead = next_frames(1 + f, h_ext, 1, 2 + f, 1, h_ext, f - old)
            halos[f - frames] = ahead
        start_all(ahead + halos[f])

    for f in (2, 3, 4):
        act_frame(x_ext, f, shift)
    message = hidden_frame(2)
    act_frame(x_ext, 5, shift)
    hidden_send(2, message)

    @pl.when(later)
    def _():
        forward(0).wait_recv()

    wait_all(prev_one)
    total = prev_total(0)
    for f in range(2):
        norm_from(f, total, old + f, gain)
    message = hidden_frame(3)
    for f in range(2):
        act_frame(x_ext, f, shift)
    hidden_send(3, message)
    hidden_send(0, hidden_frame(0))
    hidden_send(1, hidden_frame(1))

    gain, shift = vecs[3], 0.5 * vecs[4]

    def second_frame(f):
        if f < old:
            own_all(1 + f).wait_recv()
            totals[f] = own_total(1 + f)
        wait_all(halos[f])
        norm_from(2 + f, totals[f], 0, gain)
        act_frame(h_ext, 2 + f, shift)

    def joined_frame(f):
        base = x_ext[2 + f, 1:1 + rows].reshape(rows * cols, chans).astype(f32)
        joined = (base + (conv(f, w2) + vecs[5])).astype(bf16)
        j_ext[f, 1:1 + rows] = joined.reshape(rows, cols, chans)
        copies = same_rows(1 + frames + f, j_ext, 1, f, 1, j_ext, f)
        start_all(copies)
        wide = joined.astype(f32).reshape(rows, cols, chans)
        for r in range(rows):
            put_shifted(jact, f, 1 + r, wide[r])
        return copies

    totals = {}
    for f in range(old, frames):
        own_all(1 + f).wait_recv()
        totals[f] = own_total(1 + f)
        send_total(1 + f - old, totals[f])
    second_frame(2)
    second_frame(3)

    @pl.when(later)
    def _():
        forward(1).wait_recv()
        forward(2).wait_recv()

    for f in range(2):
        wait_all(halos[old + f - frames])
    for f in range(2):
        norm_from(f, prev_total(1 + f), 0, gain)
        act_frame(h_ext, f, shift)
    second_frame(0)
    load_2.wait()
    rims = [joined_frame(0)]
    second_frame(1)
    rims += [joined_frame(f) for f in range(1, frames)]

    bias = vecs[6]
    for f in range(frames):
        wait_all(rims[f])
        top = jnp.where(up_ok, j_ext[f, 0].astype(f32), 0.0)
        bottom = jnp.where(down_ok, j_ext[f, rows + 1].astype(f32), 0.0)
        put_shifted(jact, f, 0, top)
        put_shifted(jact, f, rows + 1, bottom)
        for r in range(2):
            parts = [jact[f, r + dy:r + dy + rows].reshape(rows * cols, KP) for dy in range(2)]
            made = jnp.dot(
                jnp.concatenate(parts, axis=-1), wup[r].reshape(2 * KP, chans), preferred_element_type=f32
            ) + bias
            made = made.astype(bf16).reshape(rows, cols, chans)
            for y in range(rows):
                out[f, 2 * y + r] = made[y]

    for copy, sends, _ in pending:
        pl.when(sends)(copy.wait_send)
    for slot in sent:
        own_all(slot).wait_send()

    @pl.when(first)
    def _():
        for slot in range(3):
            forward(slot).wait_send()


def solution(mesh):
    n = mesh.shape["tile"]

    def body(features, g1, s1, k1, b1, g2, s2, k2, b2, uk, ub):
        _, frames, rows, cols, chans = features.shape
        bf16, f32 = jnp.bfloat16, jnp.float32
        hbm = pl.BlockSpec(memory_space=pltpu.HBM)
        vec = lambda v: v.reshape(1, -1)
        dma = pltpu.SemaphoreType.DMA
        made = pl.pallas_call(
            functools.partial(kernel, n),
            out_shape=jax.ShapeDtypeStruct((frames, 2 * rows, cols, chans), bf16),
            in_specs=[hbm] * 11,
            out_specs=pl.BlockSpec(memory_space=pltpu.VMEM),
            scratch_shapes=[
                pltpu.VMEM((frames + 2, rows + 2, cols, chans), bf16),
                pltpu.VMEM((frames + 2, rows + 2, cols, chans), bf16),
                pltpu.VMEM((frames, rows + 2, cols, chans), bf16),
                pltpu.VMEM((frames + 2, rows + 2, cols, KP), bf16),
                pltpu.VMEM((frames, rows + 2, cols, KP), bf16),
                pltpu.VMEM((9, KP, chans), bf16),
                pltpu.VMEM((9, KP, chans), bf16),
                pltpu.VMEM((2, 2, KP, chans), bf16),
                pltpu.VMEM(uk.shape, bf16),
                pltpu.VMEM((7, 1, chans), f32),
                pltpu.VMEM((1, chans // 2), f32),
                pltpu.VMEM((frames + 2, 8, chans), f32),
                pltpu.VMEM((frames, chans, 128), bf16),
                pltpu.VMEM((frames, 128, chans), bf16),
                pltpu.VMEM((1 + frames, n, 8, 128), f32),
                pltpu.VMEM((3, 8, 128), f32),
                pltpu.VMEM((3, 8, 128), f32),
                pltpu.VMEM((rows + 2, cols + 16, chans), f32),
                dma((11,)),
                dma((1 + 2 * frames, 5)),
                dma((1 + 2 * frames, 5)),
                dma((1 + frames,)),
                dma((1 + frames,)),
                dma((3,)),
                dma((3,)),
            ],
            compiler_params=pltpu.CompilerParams(
                collective_id=0, has_side_effects=True, vmem_limit_bytes=56 * 1024 * 1024
            ),
        )(
            features[0], vec(g1), vec(s1), k1.reshape(9, 3 * chans, chans), vec(b1),
            vec(g2), vec(s2), k2.reshape(9, 3 * chans, chans), vec(b2), uk, vec(ub),
        )
        return made[None]

    return jax.shard_map(
        body,
        mesh=mesh,
        in_specs=(P(None, "tm", "tile", None, None),) + (P(),) * 10,
        out_specs=P(None, "tm", "tile", None, None),
        check_vma=False,
    )
```

profile of v0, /device:TPU:0, one launch (start us, length us, event | category | flops | bytes accessed | tf_op | source)
XLA Modules:
  0.0 41.3 jit_solution(12137243645352596291)
XLA Ops:
  0.0 39.0 %shard_map.109 = bf16[4,8,64,192]{3,2,1,0:T(8,128)(2,1)} custom-call(bf16[4,4,64,192]{3,2,1,0:T(8,128)(2,1)} %bitcast.14, f32[1,192]{1,0:T(1,128)} %bitcast.15, f32[1,192]{1,0:T(1,128)} %bitcast.16, bf16[9,576,192]{2,1,0:T(8,128)(2,1)} %bitcast.12, f32[1,192]{1,0:T(1,128)} %bitcast.17, f32[1,192]{1,0:T(1,128)} %bitcast.18, f32[1,192]{1,0:T(1,128)} %bitcast.19, ...), custom_call_target="tpu_custom_call" | custom-call | tf_op jit(solution)/shard_map/pallas_call | solution.py:358
  39.0 2.3 %copy.13 = bf16[1,4,8,64,192]{4,3,2,1,0:T(8,128)(2,1)} copy(bf16[1,4,8,64,192]{4,3,2,1,0:T(8,128)(2,1)} %bitcast.11) | data formatting | bytes 1572864
where the time goes:
time: 41.5 us; the launch traced here: 41.3 us
  Pallas kernels  39 us (94%)
  local copies, waits for them, and re-layouts  2.3 us (6%)
    pallas_call x1, Pallas kernels, body(): pl.pallas_call(functools.partial(kernel, n), out_shape=jax.ShapeDtypeStru...  39 us
    unnamed x1, local copies, waits for them, and re-layouts  2.3 us

commit v1 on v0

v1 whole, which is shorter than its diff:
```python
import functools

import jax
import jax.numpy as jnp
from jax import lax
from jax.experimental import pallas as pl
from jax.experimental.pallas import tpu as pltpu
from jax.sharding import PartitionSpec as P

MESH = pl.DeviceIdType.MESH
G = 32
EPS = 1e-06
KP = 640


def split_dot(value, picks):
    m = value.shape[0]
    high = value.astype(jnp.bfloat16).astype(jnp.float32)
    rest = value - high
    mid = rest.astype(jnp.bfloat16).astype(jnp.float32)
    low = rest - mid
    terms = jnp.concatenate([high, mid, low], axis=0).astype(jnp.bfloat16)
    made = jnp.dot(terms, picks, preferred_element_type=jnp.float32)
    return made[0:m] + made[m:2 * m] + made[2 * m:3 * m]


def kernel(
    n,
    feat, g1_h, s1_h, k1, b1_h, g2_h, s2_h, k2, b2_h, uk, ub_h,
    out,
    x_ext, h_ext, j_ext, act1, act2, jact, w1, w2, wup, ukv, vecs, ubv, norm, part, gmap, smap, stats, beside,
    loc_sem, row_send, row_recv, own_send, own_recv, prev_send, prev_recv,
):
    frames, rows, cols, chans = feat.shape
    bf16, f32 = jnp.bfloat16, jnp.float32
    tm = lax.axis_index("tm")
    tile = lax.axis_index("tile")
    up_ok = tile > 0
    down_ok = tile < n - 1
    first = tm == 0
    later = tm > 0
    above = lax.rem(tile + n - 1, n)
    below = lax.rem(tile + 1, n)
    per = chans // G
    half = chans // 2
    inverse = 1.0 / float(n * rows * cols * per)
    old = frames - 2
    pairs = ((old, frames), (0, old))

    def local(i, s, d):
        copy = pltpu.make_async_copy(s, d, loc_sem.at[i])
        copy.start()
        return copy

    load_x = local(0, feat, x_ext.at[:, pl.ds(1, rows)])

    barrier = pltpu.get_barrier_semaphore()
    for d in range(1, n):
        to = lax.rem(tile + d, n)
        pl.semaphore_signal(barrier, inc=1, device_id=(tm, to), device_id_type=MESH)
    pl.semaphore_signal(barrier, inc=1, device_id=(1 - tm, tile), device_id_type=MESH)

    load_u = local(1, uk, ukv)
    load_v = [
        local(4 + i, ref, vecs.at[i])
        for i, ref in enumerate((g1_h, s1_h, b1_h, g2_h, s2_h, b2_h))
    ]
    load_b = local(10, ub_h, ubv)
    load_1 = local(2, k1, w1.at[:, pl.ds(0, 3 * chans)])
    load_2 = local(3, k2, w2.at[:, pl.ds(0, 3 * chans)])

    pending = []

    def send_rows(slot, src, row0, f0, count, dst):
        f = pl.ds(f0, count)

        def remote(i, s, d, who):
            return pltpu.make_async_remote_copy(
                src_ref=s, dst_ref=d,
                send_sem=row_send.at[slot, i], recv_sem=row_recv.at[slot, i],
                device_id=(tm, who), device_id_type=MESH,
            )

        copies = [
            (remote(0, src.at[f, row0 + rows - 1], dst.at[f, 0], below), down_ok, up_ok),
            (remote(1, src.at[f, row0], dst.at[f, rows + 1], above), up_ok, down_ok),
        ]
        for copy, sends, _ in copies:
            pl.when(sends)(copy.start)
        pending.extend(copies)
        return copies

    def wait_rows(copies):
        for copy, _, gets in copies:
            pl.when(gets)(copy.wait_recv)

    sent = []

    def own_copy(slot, d):
        return pltpu.make_async_remote_copy(
            src_ref=stats.at[slot, 0], dst_ref=stats.at[slot, d],
            send_sem=own_send.at[slot], recv_sem=own_recv.at[slot],
            device_id=(tm, lax.rem(tile + d, n)), device_id_type=MESH)

    def own_all(slot):
        view = stats.at[slot, pl.ds(1, n - 1)]
        return pltpu.make_async_remote_copy(
            src_ref=view, dst_ref=view, send_sem=own_send.at[slot], recv_sem=own_recv.at[slot],
            device_id=(tm, below), device_id_type=MESH)

    def send_sums(slot):
        for d in range(1, n):
            own_copy(slot, d).start()
        sent.append(slot)

    def ahead(slot, ref):
        return pltpu.make_async_remote_copy(
            src_ref=ref.at[pl.ds(frames, 2)], dst_ref=ref.at[pl.ds(0, 2)],
            send_sem=prev_send.at[slot], recv_sem=prev_recv.at[slot],
            device_id=(1, tile), device_id_type=MESH)

    def put_sums(slot, flats):
        sums = [jnp.sum(v, axis=0, keepdims=True) for v in flats]
        sums += [jnp.sum(v * v, axis=0, keepdims=True) for v in flats]
        stats[slot, 0, 0:len(sums)] = split_dot(jnp.concatenate(sums, axis=0), gmap[...])

    def norm_from(slot, f0, count, gain):
        total = jnp.sum(stats[slot], axis=0)[0:2 * count]
        both = split_dot(total, smap[...]) * inverse
        mean = both[0:count]
        var = both[count:2 * count] - mean * mean
        scale = 0.5 * (lax.rsqrt(var + EPS) * gain)
        for i in range(count):
            norm[f0 + i, 0:1] = mean[i:i + 1]
            norm[f0 + i, 1:2] = scale[i:i + 1]

    def put_shifted(dst, f, r, value):
        beside[r, 8:8 + cols] = value
        left = beside[r, 7:7 + cols]
        right = beside[r, 9:9 + cols]
        dst[f, r, :, 0:chans] = left.astype(bf16)
        dst[f, r, :, chans:2 * chans] = value.astype(bf16)
        dst[f, r, :, 2 * chans:3 * chans] = right.astype(bf16)

    def act_rows(src, dst, f, which, shift):
        mean, scale = norm[f, 0:1], norm[f, 1:2]
        for r in which:
            scaled = (src[f, r].astype(f32) - mean) * scale + shift
            value = scaled + scaled * jnp.tanh(scaled)
            if r == 0:
                value = jnp.where(up_ok, value, 0.0)
            if r == rows + 1:
                value = jnp.where(down_ok, value, 0.0)
            put_shifted(dst, 2 + f, r, value)

    inner, outer = range(1, rows + 1), (0, rows + 1)

    def conv(act, w, f0, count, taps):
        parts = [
            act[f0 + i:f0 + i + count, j:j + rows].reshape(count * rows * cols, KP)
            for i in taps for j in range(3)
        ]
        return jnp.dot(
            jnp.concatenate(parts, axis=-1),
            w[3 * taps[0]:3 * taps[-1] + 3].reshape(3 * len(taps) * KP, chans),
            preferred_element_type=f32,
        )

    lane = lax.broadcasted_iota(jnp.int32, (chans, 128), 1) * per
    chan = lax.broadcasted_iota(jnp.int32, (chans, 128), 0)
    gmap[...] = jnp.where((chan >= lane) & (chan < lane + per), 1.0, 0.0).astype(bf16)
    lane = lax.broadcasted_iota(jnp.int32, (128, chans), 0) * per
    chan = lax.broadcasted_iota(jnp.int32, (128, chans), 1)
    smap[...] = jnp.where((chan >= lane) & (chan < lane + per), 1.0, 0.0).astype(bf16)
    for slot in (1, 2):
        stats[slot, 0, 4:8] = jnp.zeros((4, 128), f32)

    load_x.wait()
    put_sums(0, [x_ext[f, 1:1 + rows].reshape(rows * cols, chans).astype(f32) for f in range(frames)])
    pl.semaphore_wait(barrier, n)
    send_sums(0)
    rim_x = send_rows(0, feat, 0, 0, frames, x_ext)

    pad = KP - 3 * chans
    beside[:, 0:8] = jnp.zeros((rows + 2, 8, chans), f32)
    beside[:, 8 + cols:16 + cols] = jnp.zeros((rows + 2, 8, chans), f32)
    for act in (act1, act2):
        act[2:2 + frames, :, :, 3 * chans:KP] = jnp.zeros((frames, rows + 2, cols, pad), bf16)
    jact[:, :, :, 3 * chans:KP] = jnp.zeros((frames, rows + 2, cols, pad), bf16)
    w1[:, 3 * chans:KP] = jnp.zeros((9, pad, chans), bf16)
    w2[:, 3 * chans:KP] = jnp.zeros((9, pad, chans), bf16)
    wup[:, :, 3 * chans:KP] = jnp.zeros((2, 2, pad, chans), bf16)

    @pl.when(first)
    def _():
        for act in (act1, act2):
            act[0:2] = jnp.zeros((2, rows + 2, cols, KP), bf16)

    load_u.wait()
    for r in range(2):
        for dy in range(2):
            js = (((0,), (1, 2)) if r == 0 else ((0, 1), (2,)))[dy]
            line = [
                functools.reduce(jnp.add, [ukv[j, k].astype(f32) for j in js]) for k in range(3)
            ]
            zero = jnp.zeros_like(line[0])
            pieces = [(line[0], zero), (line[1] + line[2], line[0] + line[1]), (zero, line[2])]
            for dx, (even, odd) in enumerate(pieces):
                wup[r, dy, dx * chans:(dx + 1) * chans, 0:half] = even.astype(bf16)
                wup[r, dy, dx * chans:(dx + 1) * chans, half:chans] = odd.astype(bf16)
    for copy in load_v:
        copy.wait()
    load_b.wait()
    vecs[6, :, 0:half] = ubv[...]
    vecs[6, :, half:chans] = ubv[...]
    load_1.wait()

    own_all(0).wait_recv()
    norm_from(0, 0, frames, vecs[0])
    shift = 0.5 * vecs[1]
    for f in (2, 3, 0, 1):
        act_rows(x_ext, act1, f, inner, shift)
    wait_rows(rim_x)
    for f in (2, 3):
        act_rows(x_ext, act1, f, outer, shift)

    @pl.when(first)
    def _():
        ahead(0, act1).start()

    for f in (0, 1):
        act_rows(x_ext, act1, f, outer, shift)

    rims = []
    for slot, (f0, f1) in enumerate(pairs):
        if slot == 1:
            @pl.when(later)
            def _():
                ahead(0, act1).wait_recv()

        hidden = (conv(act1, w1, f0, f1 - f0, (0, 1, 2)) + vecs[2]).astype(bf16)
        h_ext[f0:f1, 1:1 + rows] = hidden.reshape(f1 - f0, rows, cols, chans)
        wide = hidden.astype(f32)
        put_sums(1 + slot, [wide[i * rows * cols:(i + 1) * rows * cols] for i in range(f1 - f0)])
        send_sums(1 + slot)
        rims.append(send_rows(1 + slot, h_ext, 1, f0, f1 - f0, h_ext))

    shift = 0.5 * vecs[4]

    def second(slot):
        f0, f1 = pairs[slot]
        own_all(1 + slot).wait_recv()
        norm_from(1 + slot, f0, f1 - f0, vecs[3])
        for f in range(f0, f1):
            act_rows(h_ext, act2, f, inner, shift)
        wait_rows(rims[slot])
        for f in range(f0, f1):
            act_rows(h_ext, act2, f, outer, shift)

    second(0)

    @pl.when(first)
    def _():
        ahead(1, act2).start()

    load_2.wait()
    part[0] = conv(act2, w2, 2, 1, (2,))
    part[1] = conv(act2, w2, 3, 1, (1, 2))
    second(1)

    def joined(slot, made):
        f0, f1 = pairs[slot]
        count = f1 - f0
        base = x_ext[f0:f1, 1:1 + rows].reshape(count * rows * cols, chans).astype(f32)
        value = (base + (made + vecs[5])).astype(bf16)
        j_ext[f0:f1, 1:1 + rows] = value.reshape(count, rows, cols, chans)
        copies = send_rows(3 + slot, j_ext, 1, f0, count, j_ext)
        wide = value.astype(f32).reshape(count, rows, cols, chans)
        for i in range(count):
            for r in range(rows):
                put_shifted(jact, f0 + i, 1 + r, wide[i, r])
        return copies

    made = jnp.concatenate(
        [part[0] + conv(act2, w2, 2, 1, (0, 1)), part[1] + conv(act2, w2, 3, 1, (0,))], axis=0
    )
    rims_j = [joined(0, made)]

    @pl.when(later)
    def _():
        ahead(1, act2).wait_recv()

    rims_j.append(joined(1, conv(act2, w2, 0, 2, (0, 1, 2))))

    bias = vecs[6]

    def up(slot, r, y0, y1):
        f0, f1 = pairs[slot]
        parts = [
            jact[f0:f1, r + dy + y0:r + dy + y1].reshape((f1 - f0) * (y1 - y0) * cols, KP) for dy in range(2)
        ]
        made = jnp.dot(
            jnp.concatenate(parts, axis=-1), wup[r].reshape(2 * KP, chans), preferred_element_type=f32
        ) + bias
        made = made.astype(bf16).reshape(f1 - f0, y1 - y0, cols, chans)
        for i in range(f1 - f0):
            for y in range(y0, y1):
                out[f0 + i, 2 * y + r] = made[i, y - y0]

    for slot in range(2):
        up(slot, 0, 1, rows)
        up(slot, 1, 0, rows - 1)
    for slot in range(2):
        wait_rows(rims_j[slot])
        for f in range(*pairs[slot]):
            put_shifted(jact, f, 0, jnp.where(up_ok, j_ext[f, 0].astype(f32), 0.0))
            put_shifted(jact, f, rows + 1, jnp.where(down_ok, j_ext[f, rows + 1].astype(f32), 0.0))
        up(slot, 0, 0, 1)
        up(slot, 1, rows - 1, rows)

    for copy, sends, _ in pending:
        pl.when(sends)(copy.wait_send)
    for slot in sent:
        own_all(slot).wait_send()

    @pl.when(first)
    def _():
        ahead(0, act1).wait_send()
        ahead(1, act2).wait_send()


def solution(mesh):
    n = mesh.shape["tile"]

    def body(features, g1, s1, k1, b1, g2, s2, k2, b2, uk, ub):
        _, frames, rows, cols, chans = features.shape
        bf16, f32 = jnp.bfloat16, jnp.float32
        hbm = pl.BlockSpec(memory_space=pltpu.HBM)
        vec = lambda v: v.reshape(1, -1)
        dma = pltpu.SemaphoreType.DMA
        made = pl.pallas_call(
            functools.partial(kernel, n),
            out_shape=pltpu.VMEM((frames, 2 * rows, cols, chans), bf16),
            in_specs=[hbm] * 11,
            out_specs=pl.BlockSpec(memory_space=pltpu.VMEM),
            scratch_shapes=[
                pltpu.VMEM((frames, rows + 2, cols, chans), bf16),
                pltpu.VMEM((frames, rows + 2, cols, chans), bf16),
                pltpu.VMEM((frames, rows + 2, cols, chans), bf16),
                pltpu.VMEM((frames + 2, rows + 2, cols, KP), bf16),
                pltpu.VMEM((frames + 2, rows + 2, cols, KP), bf16),
                pltpu.VMEM((frames, rows + 2, cols, KP), bf16),
                pltpu.VMEM((9, KP, chans), bf16),
                pltpu.VMEM((9, KP, chans), bf16),
                pltpu.VMEM((2, 2, KP, chans), bf16),
                pltpu.VMEM(uk.shape, bf16),
                pltpu.VMEM((7, 1, chans), f32),
                pltpu.VMEM((1, chans // 2), f32),
                pltpu.VMEM((frames, 8, chans), f32),
                pltpu.VMEM((2, rows * cols, chans), f32),
                pltpu.VMEM((chans, 128), bf16),
                pltpu.VMEM((128, chans), bf16),
                pltpu.VMEM((3, n, 8, 128), f32),
                pltpu.VMEM((rows + 2, cols + 16, chans), f32),
                dma((11,)),
                dma((5, 2)),
                dma((5, 2)),
                dma((3,)),
                dma((3,)),
                dma((2,)),
                dma((2,)),
            ],
            compiler_params=pltpu.CompilerParams(
                collective_id=0, has_side_effects=True, vmem_limit_bytes=56 * 1024 * 1024
            ),
        )(
            features[0], vec(g1), vec(s1), k1.reshape(9, 3 * chans, chans), vec(b1),
            vec(g2), vec(s2), k2.reshape(9, 3 * chans, chans), vec(b2), uk, vec(ub),
        )
        return made[None]

    return jax.shard_map(
        body,
        mesh=mesh,
        in_specs=(P(None, "tm", "tile", None, None),) + (P(),) * 10,
        out_specs=P(None, "tm", "tile", None, None),
        check_vma=False,
    )
```

time: 41.5 us -> 36.9 us (0.89)
  Pallas kernels: 39 us -> 35.8 us
  local copies, waits for them, and re-layouts: 2.3 us -> 0.97 us
    pallas_call x1, Pallas kernels: 39 us -> 35.8 us  [body(): pl.pallas_call(functools.partial(kernel, n), out_shape=pltpu.VMEM((frames...]
    unnamed x1, local copies, waits for them, and re-layouts: 2.3 us -> 0.97 us
where the time goes in v1:
time: 36.9 us; the launch traced here: 36.8 us
  Pallas kernels  35.8 us (97%)
  local copies, waits for them, and re-layouts  0.97 us (3%)
    pallas_call x1, Pallas kernels, body(): pl.pallas_call(functools.partial(kernel, n), out_shape=pltpu.VMEM((frames...  35.8 us
    unnamed x1, local copies, waits for them, and re-layouts  0.97 us

profile of v1, /device:TPU:0, one launch (start us, length us, event | category | flops | bytes accessed | tf_op | source)
XLA Modules:
  0.0 36.8 jit_solution(1713702672632816887)
XLA Ops:
  0.0 35.8 %shard_map.109 = bf16[4,8,64,192]{3,2,1,0:T(8,128)(2,1)S(1)} custom-call(bf16[4,4,64,192]{3,2,1,0:T(8,128)(2,1)} %bitcast.14, f32[1,192]{1,0:T(1,128)} %bitcast.15, f32[1,192]{1,0:T(1,128)} %bitcast.16, bf16[9,576,192]{2,1,0:T(8,128)(2,1)} %bitcast.12, f32[1,192]{1,0:T(1,128)} %bitcast.17, f32[1,192]{1,0:T(1,128)} %bitcast.18, f32[1,192]{1,0:T(1,128)} %bitcast.19, ...), custom_call_target="tpu_custom_call" | custom-call | tf_op jit(solution)/shard_map/pallas_call | solution.py:341
  35.8 1.0 %copy.13 = bf16[1,4,8,64,192]{4,3,2,1,0:T(8,128)(2,1)} copy(bf16[1,4,8,64,192]{4,3,2,1,0:T(8,128)(2,1)S(1)} %bitcast.11) | data formatting | bytes 1572864

commit v2 on v1

v2 whole, which is shorter than its diff:
```python
import functools

import jax
import jax.numpy as jnp
from jax import lax
from jax.experimental import pallas as pl
from jax.experimental.pallas import tpu as pltpu
from jax.sharding import PartitionSpec as P

MESH = pl.DeviceIdType.MESH
G = 32
EPS = 1e-06
KP = 640


def split_dot(value, picks):
    m = value.shape[0]
    high = value.astype(jnp.bfloat16).astype(jnp.float32)
    rest = value - high
    mid = rest.astype(jnp.bfloat16).astype(jnp.float32)
    low = rest - mid
    terms = jnp.concatenate([high, mid, low], axis=0).astype(jnp.bfloat16)
    made = jnp.dot(terms, picks, preferred_element_type=jnp.float32)
    return made[0:m] + made[m:2 * m] + made[2 * m:3 * m]


def kernel(
    n,
    feat, g1_h, s1_h, k1, b1_h, g2_h, s2_h, k2, b2_h, uk, ub_h,
    out,
    x_own, h_own, act1, act2, jact, w1, w2, wup, ukv, vecs, ubv, norm, sums, gmap, smap, stats, rim_out, rim_in, beside,
    loc_sem, row_send, row_recv, own_send, own_recv, prev_send, prev_recv,
):
    frames, rows, cols, chans = feat.shape
    bf16, f32 = jnp.bfloat16, jnp.float32
    tm = lax.axis_index("tm")
    tile = lax.axis_index("tile")
    up_ok = tile > 0
    down_ok = tile < n - 1
    first = tm == 0
    later = tm > 0
    above = lax.rem(tile + n - 1, n)
    below = lax.rem(tile + 1, n)
    per = chans // G
    half = chans // 2
    inverse = 1.0 / float(n * rows * cols * per)
    old = frames - 2
    pairs = ((old, frames), (0, old))

    def local(i, s, d):
        copy = pltpu.make_async_copy(s, d, loc_sem.at[i])
        copy.start()
        return copy

    load_x = local(0, feat, x_own)

    barrier = pltpu.get_barrier_semaphore()
    for d in range(1, n):
        to = lax.rem(tile + d, n)
        pl.semaphore_signal(barrier, inc=1, device_id=(tm, to), device_id_type=MESH)
    pl.semaphore_signal(barrier, inc=1, device_id=(1 - tm, tile), device_id_type=MESH)

    load_u = local(1, uk, ukv)
    load_v = [
        local(4 + i, ref, vecs.at[i])
        for i, ref in enumerate((g1_h, s1_h, b1_h, g2_h, s2_h, b2_h))
    ]
    load_b = local(10, ub_h, ubv)
    load_1 = local(2, k1, w1.at[:, pl.ds(0, 3 * chans)])
    load_2 = local(3, k2, w2.at[:, pl.ds(0, 3 * chans)])

    alone = pl.when(tile >= 0)

    pending = []

    def pack(k, d, f, row):
        low = cols // 2
        side = chans - 128
        rim_out[k, d, f, 0:cols] = row[:, 0:128]
        rim_out[k, d, f, cols:cols + low, 0:side] = row[0:low, 128:chans]
        rim_out[k, d, f, cols:cols + low, 64:64 + side] = row[low:cols, 128:chans]

    def unpack(k, d, f):
        low = cols // 2
        side = chans - 128
        edge = rim_in[k, d, f].astype(f32)
        rest = jnp.concatenate([edge[cols:cols + low, 0:side], edge[cols:cols + low, 64:64 + side]], axis=0)
        return jnp.concatenate([edge[0:cols], rest], axis=-1)

    def send_rows(k, slot, f0, f1):
        f = pl.ds(f0, f1 - f0)

        def remote(d, who):
            return pltpu.make_async_remote_copy(
                src_ref=rim_out.at[k, d, f], dst_ref=rim_in.at[k, d, f],
                send_sem=row_send.at[slot, d], recv_sem=row_recv.at[slot, d],
                device_id=(tm, who), device_id_type=MESH,
            )

        copies = [(remote(0, below), down_ok, up_ok), (remote(1, above), up_ok, down_ok)]
        for copy, sends, _ in copies:
            pl.when(sends)(copy.start)
        pending.extend(copies)
        return copies

    def wait_rows(copies):
        for copy, _, gets in copies:
            pl.when(gets)(copy.wait_recv)

    sent = []

    def own_copy(slot, d):
        return pltpu.make_async_remote_copy(
            src_ref=stats.at[slot, 0, pl.ds(0, 2)], dst_ref=stats.at[slot, d, pl.ds(0, 2)],
            send_sem=own_send.at[slot], recv_sem=own_recv.at[slot],
            device_id=(tm, lax.rem(tile + d, n)), device_id_type=MESH)

    def own_all(slot):
        view = stats.at[slot, pl.ds(1, n - 1), pl.ds(0, 2)]
        return pltpu.make_async_remote_copy(
            src_ref=view, dst_ref=view, send_sem=own_send.at[slot], recv_sem=own_recv.at[slot],
            device_id=(tm, below), device_id_type=MESH)

    def send_sums(slot):
        for d in range(1, n):
            own_copy(slot, d).start()
        sent.append(slot)

    def ahead(k, part, ref):
        lines = (pl.ds(1, rows), 0, rows + 1)[part]
        return pltpu.make_async_remote_copy(
            src_ref=ref.at[pl.ds(frames, 2), lines], dst_ref=ref.at[pl.ds(0, 2), lines],
            send_sem=prev_send.at[k, part], recv_sem=prev_recv.at[k, part],
            device_id=(1, tile), device_id_type=MESH)

    def give(k, parts, ref):
        @pl.when(first)
        def _():
            for part in parts:
                ahead(k, part, ref).start()

    def take(k, parts, ref):
        @pl.when(later)
        def _():
            for part in parts:
                ahead(k, part, ref).wait_recv()

    block_of = lax.broadcasted_iota(jnp.int32, (frames, 128), 1) // G
    block = jnp.where(block_of == lax.broadcasted_iota(jnp.int32, (frames, 128), 0), 1.0, 0.0)

    def put_sums(slot):
        @alone
        def _():
            made = split_dot(sums[...], gmap[...])
            for i in range(2):
                stats[slot, 0, i:i + 1] = jnp.sum(made[i * frames:(i + 1) * frames] * block, axis=0, keepdims=True)

    def add_sums(f, value, fresh):
        for i, v in enumerate((value, value * value)):
            line = slice(i * frames + f, i * frames + f + 1)
            total = jnp.sum(v, axis=0, keepdims=True)
            sums[line] = total if fresh else sums[line] + total

    def norm_from(slot, gain):
        @alone
        def _():
            total = jnp.sum(stats[slot, :, 0:2], axis=0)
            spread = jnp.concatenate([total[0:1] * block, total[1:2] * block], axis=0)
            both = split_dot(spread, smap[...]) * inverse
            mean = both[0:frames]
            var = both[frames:2 * frames] - mean * mean
            norm[0:frames] = mean
            norm[8:8 + frames] = 0.5 * (lax.rsqrt(var + EPS) * gain)

    def put_shifted(dst, f, r, value):
        beside[r, 8:8 + cols] = value
        left = beside[r, 7:7 + cols]
        right = beside[r, 9:9 + cols]
        dst[f, r, :, 0:chans] = left.astype(bf16)
        dst[f, r, :, chans:2 * chans] = value.astype(bf16)
        dst[f, r, :, 2 * chans:3 * chans] = right.astype(bf16)

    def act_row(dst, f, r, value, shift, ok=None):
        scaled = (value - norm[f:f + 1]) * norm[8 + f:9 + f] + shift
        made = scaled + scaled * jnp.tanh(scaled)
        if ok is not None:
            made = jnp.where(ok, made, 0.0)
        put_shifted(dst, 2 + f, r, made)

    def act_inner(src, dst, f, shift):
        for r in range(rows):
            act_row(dst, f, 1 + r, src[f, r].astype(f32), shift)

    def act_outer(k, dst, f, shift):
        act_row(dst, f, 0, unpack(k, 0, f), shift, up_ok)
        act_row(dst, f, rows + 1, unpack(k, 1, f), shift, down_ok)

    inner, outer = tuple(range(1, rows - 1)), (0, rows - 1)

    def lines_of(ref, f0, f1, which, j):
        if which == inner:
            return ref[f0:f1, 1 + j:rows - 1 + j]
        return jnp.concatenate([ref[f0:f1, y + j:y + j + 1] for y in which], axis=1)

    def conv(act, w, pair, which):
        f0, f1 = pair
        m = (f1 - f0) * len(which) * cols
        parts = [
            lines_of(act, f0 + i, f1 + i, which, j).reshape(m, KP) for i in range(3) for j in range(3)
        ]
        return jnp.dot(
            jnp.concatenate(parts, axis=-1), w[...].reshape(9 * KP, chans), preferred_element_type=f32
        )

    lane = lax.broadcasted_iota(jnp.int32, (chans, 128), 1) % G
    chan = lax.broadcasted_iota(jnp.int32, (chans, 128), 0) // per
    gmap[...] = jnp.where(lane == chan, 1.0, 0.0).astype(bf16)
    lane = lax.broadcasted_iota(jnp.int32, (128, chans), 0) % G
    chan = lax.broadcasted_iota(jnp.int32, (128, chans), 1) // per
    smap[...] = jnp.where(lane == chan, 1.0, 0.0).astype(bf16)

    load_x.wait()
    for f in range(frames):
        add_sums(f, x_own[f].reshape(rows * cols, chans).astype(f32), True)
    put_sums(0)
    for f in range(frames):
        pack(0, 0, f, x_own[f, rows - 1])
        pack(0, 1, f, x_own[f, 0])
    pl.semaphore_wait(barrier, n)
    send_sums(0)
    rim_x = send_rows(0, 0, 0, frames)

    pad = KP - 3 * chans
    beside[:, 0:8] = jnp.zeros((rows + 2, 8, chans), f32)
    beside[:, 8 + cols:16 + cols] = jnp.zeros((rows + 2, 8, chans), f32)
    for act in (act1, act2):
        act[2:2 + frames, :, :, 3 * chans:KP] = jnp.zeros((frames, rows + 2, cols, pad), bf16)
    jact[:, :, :, 3 * chans:KP] = jnp.zeros((frames, rows + 2, cols, pad), bf16)
    w1[:, 3 * chans:KP] = jnp.zeros((9, pad, chans), bf16)
    w2[:, 3 * chans:KP] = jnp.zeros((9, pad, chans), bf16)
    wup[:, :, 3 * chans:KP] = jnp.zeros((2, 2, pad, chans), bf16)

    @pl.when(first)
    def _():
        for act in (act1, act2):
            act[0:2] = jnp.zeros((2, rows + 2, cols, KP), bf16)

    load_u.wait()
    for r in range(2):
        for dy in range(2):
            js = (((0,), (1, 2)) if r == 0 else ((0, 1), (2,)))[dy]
            line = [
                functools.reduce(jnp.add, [ukv[j, k].astype(f32) for j in js]) for k in range(3)
            ]
            zero = jnp.zeros_like(line[0])
            pieces = [(line[0], zero), (line[1] + line[2], line[0] + line[1]), (zero, line[2])]
            for dx, (even, odd) in enumerate(pieces):
                wup[r, dy, dx * chans:(dx + 1) * chans, 0:half] = even.astype(bf16)
                wup[r, dy, dx * chans:(dx + 1) * chans, half:chans] = odd.astype(bf16)
    for copy in load_v:
        copy.wait()
    load_b.wait()
    vecs[6, :, 0:half] = ubv[...]
    vecs[6, :, half:chans] = ubv[...]
    load_1.wait()
    load_2.wait()

    def stage(k, src, act, gain, shift, rims, piece, after):
        own_all(k).wait_recv()
        norm_from(k, gain)
        for f in range(*pairs[0]):
            act_inner(src, act, f, shift)
        give(k, (0,), act)
        for f in range(*pairs[1]):
            act_inner(src, act, f, shift)
        alone(functools.partial(piece, pairs[0], inner))
        take(k, (0,), act)
        alone(functools.partial(piece, pairs[1], inner))
        for copies in rims:
            wait_rows(copies)
        for f in range(*pairs[0]):
            act_outer(k, act, f, shift)
        give(k, (1, 2), act)
        for f in range(*pairs[1]):
            act_outer(k, act, f, shift)
        alone(functools.partial(piece, pairs[0], outer))
        after(0)
        take(k, (1, 2), act)
        alone(functools.partial(piece, pairs[1], outer))
        after(1)

    def each(pair, which):
        at = 0
        for f in range(*pair):
            for y in which:
                yield f, y, slice(at * cols, (at + 1) * cols)
                at += 1

    def hidden_piece(pair, which):
        made = (conv(act1, w1, pair, which) + vecs[2]).astype(bf16)
        wide = made.astype(f32)
        m = len(which) * cols
        for f in range(*pair):
            add_sums(f, wide[(f - pair[0]) * m:(f - pair[0] + 1) * m], which == inner)
        for f, y, at in each(pair, which):
            h_own[f, y] = made[at]
            if y == rows - 1:
                pack(1, 0, f, made[at])
            if y == 0:
                pack(1, 1, f, made[at])

    rim_h, rim_j = [], []

    def hidden_after(slot):
        if slot == 1:
            put_sums(1)
            send_sums(1)
        rim_h.append(send_rows(1, 1 + slot, *pairs[slot]))

    def joined_piece(pair, which):
        base = lines_of(x_own, pair[0], pair[1], which, 0) if which == outer else x_own[pair[0]:pair[1], 1:rows - 1]
        base = base.reshape(-1, chans).astype(f32)
        made = (base + (conv(act2, w2, pair, which) + vecs[5])).astype(bf16)
        wide = made.astype(f32)
        for f, y, at in each(pair, which):
            if y == rows - 1:
                pack(2, 0, f, made[at])
            if y == 0:
                pack(2, 1, f, made[at])
            put_shifted(jact, f, 1 + y, wide[at])

    def joined_after(slot):
        rim_j.append(send_rows(2, 3 + slot, *pairs[slot]))

    stage(0, x_own, act1, vecs[0], 0.5 * vecs[1], [rim_x], hidden_piece, hidden_after)
    stage(1, h_own, act2, vecs[3], 0.5 * vecs[4], rim_h, joined_piece, joined_after)

    def up(pair, r, y0, y1):
        f0, f1 = pair
        parts = [
            jact[f0:f1, r + dy + y0:r + dy + y1].reshape((f1 - f0) * (y1 - y0) * cols, KP) for dy in range(2)
        ]
        made = jnp.dot(
            jnp.concatenate(parts, axis=-1), wup[r].reshape(2 * KP, chans), preferred_element_type=f32
        ) + vecs[6]
        made = made.astype(bf16).reshape(f1 - f0, y1 - y0, cols, chans)
        for i in range(f1 - f0):
            for y in range(y0, y1):
                out[f0 + i, 2 * y + r] = made[i, y - y0]

    @alone
    def _():
        up((0, frames), 0, 1, rows)

    @alone
    def _():
        up((0, frames), 1, 0, rows - 1)

    for slot in range(2):
        wait_rows(rim_j[slot])
        for f in range(*pairs[slot]):
            put_shifted(jact, f, 0, jnp.where(up_ok, unpack(2, 0, f), 0.0))
            put_shifted(jact, f, rows + 1, jnp.where(down_ok, unpack(2, 1, f), 0.0))

        @alone
        def _():
            up(pairs[slot], 0, 0, 1)
            up(pairs[slot], 1, rows - 1, rows)

    for copy, sends, _ in pending:
        pl.when(sends)(copy.wait_send)
    for slot in sent:
        own_all(slot).wait_send()

    @pl.when(first)
    def _():
        for k, act in enumerate((act1, act2)):
            for part in range(3):
                ahead(k, part, act).wait_send()


def solution(mesh):
    n = mesh.shape["tile"]

    def body(features, g1, s1, k1, b1, g2, s2, k2, b2, uk, ub):
        _, frames, rows, cols, chans = features.shape
        bf16, f32 = jnp.bfloat16, jnp.float32
        hbm = pl.BlockSpec(memory_space=pltpu.HBM)
        vec = lambda v: v.reshape(1, -1)
        dma = pltpu.SemaphoreType.DMA
        made = pl.pallas_call(
            functools.partial(kernel, n),
            out_shape=pltpu.VMEM((frames, 2 * rows, cols, chans), bf16),
            in_specs=[hbm] * 11,
            out_specs=pl.BlockSpec(memory_space=pltpu.VMEM),
            scratch_shapes=[
                pltpu.VMEM((frames, rows, cols, chans), bf16),
                pltpu.VMEM((frames, rows, cols, chans), bf16),
                pltpu.VMEM((frames + 2, rows + 2, cols, KP), bf16),
                pltpu.VMEM((frames + 2, rows + 2, cols, KP), bf16),
                pltpu.VMEM((frames, rows + 2, cols, KP), bf16),
                pltpu.VMEM((9, KP, chans), bf16),
                pltpu.VMEM((9, KP, chans), bf16),
                pltpu.VMEM((2, 2, KP, chans), bf16),
                pltpu.VMEM(uk.shape, bf16),
                pltpu.VMEM((7, 1, chans), f32),
                pltpu.VMEM((1, chans // 2), f32),
                pltpu.VMEM((16, chans), f32),
                pltpu.VMEM((2 * frames, chans), f32),
                pltpu.VMEM((chans, 128), bf16),
                pltpu.VMEM((128, chans), bf16),
                pltpu.VMEM((2, n, 8, 128), f32),
                pltpu.VMEM((3, 2, frames, cols + cols // 2, 128), bf16),
                pltpu.VMEM((3, 2, frames, cols + cols // 2, 128), bf16),
                pltpu.VMEM((rows + 2, cols + 16, chans), f32),
                dma((11,)),
                dma((5, 2)),
                dma((5, 2)),
                dma((2,)),
                dma((2,)),
                dma((2, 3)),
                dma((2, 3)),
            ],
            compiler_params=pltpu.CompilerParams(
                collective_id=0, has_side_effects=True, vmem_limit_bytes=56 * 1024 * 1024
            ),
        )(
            features[0], vec(g1), vec(s1), k1.reshape(9, 3 * chans, chans), vec(b1),
            vec(g2), vec(s2), k2.reshape(9, 3 * chans, chans), vec(b2), uk, vec(ub),
        )
        return made[None]

    return jax.shard_map(
        body,
        mesh=mesh,
        in_specs=(P(None, "tm", "tile", None, None),) + (P(),) * 10,
        out_specs=P(None, "tm", "tile", None, None),
        check_vma=False,
    )
```

time: 36.9 us -> 33.5 us (0.908)
  Pallas kernels: 35.8 us -> 32.3 us
    pallas_call x1, Pallas kernels: 35.8 us -> 32.3 us  [body(): pl.pallas_call(functools.partial(kernel, n), out_shape=pltpu.VMEM((frames...]
where the time goes in v2:
time: 33.5 us; the launch traced here: 33.3 us
  Pallas kernels  32.3 us (96%)
  local copies, waits for them, and re-layouts  0.97 us (3%)
    pallas_call x1, Pallas kernels, body(): pl.pallas_call(functools.partial(kernel, n), out_shape=pltpu.VMEM((frames...  32.3 us
    unnamed x1, local copies, waits for them, and re-layouts  0.97 us

profile of v2, /device:TPU:0, one launch (start us, length us, event | category | flops | bytes accessed | tf_op | source)
XLA Modules:
  0.0 33.3 jit_solution(1040613509577374019)
XLA Ops:
  0.0 32.3 %shard_map.109 = bf16[4,8,64,192]{3,2,1,0:T(8,128)(2,1)S(1)} custom-call(bf16[4,4,64,192]{3,2,1,0:T(8,128)(2,1)} %bitcast.14, f32[1,192]{1,0:T(1,128)} %bitcast.15, f32[1,192]{1,0:T(1,128)} %bitcast.16, bf16[9,576,192]{2,1,0:T(8,128)(2,1)} %bitcast.12, f32[1,192]{1,0:T(1,128)} %bitcast.17, f32[1,192]{1,0:T(1,128)} %bitcast.18, f32[1,192]{1,0:T(1,128)} %bitcast.19, ...), custom_call_target="tpu_custom_call" | custom-call | tf_op jit(solution)/shard_map/pallas_call | solution.py:391
  32.3 1.0 %copy.13 = bf16[1,4,8,64,192]{4,3,2,1,0:T(8,128)(2,1)} copy(bf16[1,4,8,64,192]{4,3,2,1,0:T(8,128)(2,1)S(1)} %bitcast.11) | data formatting | bytes 1572864

commit v3 on v2

--- a/solution.py
+++ b/solution.py
@@ -266,28 +266,48 @@
     load_2.wait()
 
     def stage(k, src, act, gain, shift, rims, piece, after):
+        def outer_rows(pair):
+            for f in range(*pair):
+                act_outer(k, act, f, shift)
+
         own_all(k).wait_recv()
         norm_from(k, gain)
         for f in range(*pairs[0]):
             act_inner(src, act, f, shift)
         give(k, (0,), act)
+        if k == 1:
+            for copies in rims:
+                wait_rows(copies)
+            outer_rows(pairs[0])
+            give(k, (1, 2), act)
         for f in range(*pairs[1]):
             act_inner(src, act, f, shift)
-        alone(functools.partial(piece, pairs[0], inner))
-        take(k, (0,), act)
-        alone(functools.partial(piece, pairs[1], inner))
-        for copies in rims:
-            wait_rows(copies)
-        for f in range(*pairs[0]):
-            act_outer(k, act, f, shift)
-        give(k, (1, 2), act)
-        for f in range(*pairs[1]):
-            act_outer(k, act, f, shift)
+
+        @alone
+        def _():
+            piece(pairs[0], inner)
+            if k == 1:
+                outer_rows(pairs[1])
+
+        if k == 0:
+            for copies in rims:
+                wait_rows(copies)
+            outer_rows(pairs[0])
+            give(k, (1, 2), act)
+            outer_rows(pairs[1])
         alone(functools.partial(piece, pairs[0], outer))
         after(0)
-        take(k, (1, 2), act)
-        alone(functools.partial(piece, pairs[1], outer))
-        after(1)
+        if k == 0:
+            take(k, (0,), act)
+            alone(functools.partial(piece, pairs[1], inner))
+            take(k, (1, 2), act)
+            alone(functools.partial(piece, pairs[1], outer))
+            after(1)
+        else:
+            take(k, (0, 1, 2), act)
+            alone(functools.partial(piece, pairs[1], outer))
+            after(1)
+            alone(functools.partial(piece, pairs[1], inner))
 
     def each(pair, which):
         at = 0

time: 33.5 us -> 31.1 us (0.928)
  Pallas kernels: 32.3 us -> 30 us
    pallas_call x1, Pallas kernels: 32.3 us -> 30 us  [body(): pl.pallas_call(functools.partial(kernel, n), out_shape=pltpu.VMEM((frames...]
where the time goes in v3:
time: 31.1 us; the launch traced here: 31 us
  Pallas kernels  30 us (96%)
  local copies, waits for them, and re-layouts  0.97 us (3%)
    pallas_call x1, Pallas kernels, body(): pl.pallas_call(functools.partial(kernel, n), out_shape=pltpu.VMEM((frames...  30 us
    unnamed x1, local copies, waits for them, and re-layouts  0.97 us

profile of v3, /device:TPU:0, one launch (start us, length us, event | category | flops | bytes accessed | tf_op | source)
XLA Modules:
  0.0 31.0 jit_solution(6465844487281479573)
XLA Ops:
  0.0 30.0 %shard_map.109 = bf16[4,8,64,192]{3,2,1,0:T(8,128)(2,1)S(1)} custom-call(bf16[4,4,64,192]{3,2,1,0:T(8,128)(2,1)} %bitcast.14, f32[1,192]{1,0:T(1,128)} %bitcast.15, f32[1,192]{1,0:T(1,128)} %bitcast.16, bf16[9,576,192]{2,1,0:T(8,128)(2,1)} %bitcast.12, f32[1,192]{1,0:T(1,128)} %bitcast.17, f32[1,192]{1,0:T(1,128)} %bitcast.18, f32[1,192]{1,0:T(1,128)} %bitcast.19, ...), custom_call_target="tpu_custom_call" | custom-call | tf_op jit(solution)/shard_map/pallas_call | solution.py:411
  30.0 1.0 %copy.13 = bf16[1,4,8,64,192]{4,3,2,1,0:T(8,128)(2,1)} copy(bf16[1,4,8,64,192]{4,3,2,1,0:T(8,128)(2,1)S(1)} %bitcast.11) | data formatting | bytes 1572864

commit v4 on v2

--- a/solution.py
+++ b/solution.py
@@ -28,7 +28,7 @@
     n,
     feat, g1_h, s1_h, k1, b1_h, g2_h, s2_h, k2, b2_h, uk, ub_h,
     out,
-    x_own, h_own, act1, act2, jact, w1, w2, wup, ukv, vecs, ubv, norm, sums, gmap, smap, stats, rim_out, rim_in, beside,
+    x_own, h_own, act1, act2, jact, w1, w2, wup, ukv, vecs, ubv, norm, norm_out, norm_in, sums, gmap, smap, stats, rim_out, rim_in, rim_prev, beside,
     loc_sem, row_send, row_recv, own_send, own_recv, prev_send, prev_recv,
 ):
     frames, rows, cols, chans = feat.shape
@@ -52,7 +52,7 @@
         copy.start()
         return copy
 
-    load_x = local(0, feat, x_own)
+    load_x = local(0, feat, x_own.at[pl.ds(2, frames)])
 
     barrier = pltpu.get_barrier_semaphore()
     for d in range(1, n):
@@ -80,10 +80,10 @@
         rim_out[k, d, f, cols:cols + low, 0:side] = row[0:low, 128:chans]
         rim_out[k, d, f, cols:cols + low, 64:64 + side] = row[low:cols, 128:chans]
 
-    def unpack(k, d, f):
+    def unpack(edge):
         low = cols // 2
         side = chans - 128
-        edge = rim_in[k, d, f].astype(f32)
+        edge = edge.astype(f32)
         rest = jnp.concatenate([edge[cols:cols + low, 0:side], edge[cols:cols + low, 64:64 + side]], axis=0)
         return jnp.concatenate([edge[0:cols], rest], axis=-1)
 
@@ -126,24 +126,22 @@
             own_copy(slot, d).start()
         sent.append(slot)
 
-    def ahead(k, part, ref):
-        lines = (pl.ds(1, rows), 0, rows + 1)[part]
+    def ahead(k, part):
+        held = feat.at[pl.ds(old, 2)] if k == 0 else h_own.at[pl.ds(frames, 2)]
+        source, target = (
+            (held, (x_own, h_own)[k].at[pl.ds(0, 2)]),
+            (norm_out.at[k], norm_in.at[k]),
+            (rim_in.at[k, pl.ds(0, 2), pl.ds(old, 2)], rim_prev.at[k]),
+        )[part]
         return pltpu.make_async_remote_copy(
-            src_ref=ref.at[pl.ds(frames, 2), lines], dst_ref=ref.at[pl.ds(0, 2), lines],
+            src_ref=source, dst_ref=target,
             send_sem=prev_send.at[k, part], recv_sem=prev_recv.at[k, part],
             device_id=(1, tile), device_id_type=MESH)
 
-    def give(k, parts, ref):
+    def give(k, part):
         @pl.when(first)
         def _():
-            for part in parts:
-                ahead(k, part, ref).start()
-
-    def take(k, parts, ref):
-        @pl.when(later)
-        def _():
-            for part in parts:
-                ahead(k, part, ref).wait_recv()
+            ahead(k, part).start()
 
     block_of = lax.broadcasted_iota(jnp.int32, (frames, 128), 1) // G
     block = jnp.where(block_of == lax.broadcasted_iota(jnp.int32, (frames, 128), 0), 1.0, 0.0)
@@ -169,8 +167,11 @@
             both = split_dot(spread, smap[...]) * inverse
             mean = both[0:frames]
             var = both[frames:2 * frames] - mean * mean
+            scale = 0.5 * (lax.rsqrt(var + EPS) * gain)
             norm[0:frames] = mean
-            norm[8:8 + frames] = 0.5 * (lax.rsqrt(var + EPS) * gain)
+            norm[8:8 + frames] = scale
+            norm_out[slot, 0:2] = mean[old:frames]
+            norm_out[slot, 2:4] = scale[old:frames]
 
     def put_shifted(dst, f, r, value):
         beside[r, 8:8 + cols] = value
@@ -180,20 +181,20 @@
         dst[f, r, :, chans:2 * chans] = value.astype(bf16)
         dst[f, r, :, 2 * chans:3 * chans] = right.astype(bf16)
 
-    def act_row(dst, f, r, value, shift, ok=None):
-        scaled = (value - norm[f:f + 1]) * norm[8 + f:9 + f] + shift
+    def act_row(dst, f, r, value, mean, scale, shift, ok=None):
+        scaled = (value - mean) * scale + shift
         made = scaled + scaled * jnp.tanh(scaled)
         if ok is not None:
             made = jnp.where(ok, made, 0.0)
-        put_shifted(dst, 2 + f, r, made)
-
-    def act_inner(src, dst, f, shift):
+        put_shifted(dst, f, r, made)
+
+    def act_inner(src, dst, f, mean, scale, shift):
         for r in range(rows):
-            act_row(dst, f, 1 + r, src[f, r].astype(f32), shift)
-
-    def act_outer(k, dst, f, shift):
-        act_row(dst, f, 0, unpack(k, 0, f), shift, up_ok)
-        act_row(dst, f, rows + 1, unpack(k, 1, f), shift, down_ok)
+            act_row(dst, f, 1 + r, src[f, r].astype(f32), mean, scale, shift)
+
+    def act_outer(top, bottom, dst, f, mean, scale, shift):
+        act_row(dst, f, 0, unpack(top), mean, scale, shift, up_ok)
+        act_row(dst, f, rows + 1, unpack(bottom), mean, scale, shift, down_ok)
 
     inner, outer = tuple(range(1, rows - 1)), (0, rows - 1)
 
@@ -221,14 +222,15 @@
 
     load_x.wait()
     for f in range(frames):
-        add_sums(f, x_own[f].reshape(rows * cols, chans).astype(f32), True)
+        add_sums(f, x_own[2 + f].reshape(rows * cols, chans).astype(f32), True)
     put_sums(0)
     for f in range(frames):
-        pack(0, 0, f, x_own[f, rows - 1])
-        pack(0, 1, f, x_own[f, 0])
+        pack(0, 0, f, x_own[2 + f, rows - 1])
+        pack(0, 1, f, x_own[2 + f, 0])
     pl.semaphore_wait(barrier, n)
     send_sums(0)
     rim_x = send_rows(0, 0, 0, frames)
+    give(0, 0)
 
     pad = KP - 3 * chans
     beside[:, 0:8] = jnp.zeros((rows + 2, 8, chans), f32)
@@ -266,28 +268,41 @@
     load_2.wait()
 
     def stage(k, src, act, gain, shift, rims, piece, after):
+        def inner_rows():
+            for f in range(frames):
+                act_inner(src, act, 2 + f, norm[f:f + 1], norm[8 + f:9 + f], shift)
+
+        def outer_rows():
+            for copies in rims:
+                wait_rows(copies)
+            give(k, 2)
+            for f in range(frames):
+                act_outer(rim_in[k, 0, f], rim_in[k, 1, f], act, 2 + f, norm[f:f + 1], norm[8 + f:9 + f], shift)
+
         own_all(k).wait_recv()
         norm_from(k, gain)
-        for f in range(*pairs[0]):
-            act_inner(src, act, f, shift)
-        give(k, (0,), act)
-        for f in range(*pairs[1]):
-            act_inner(src, act, f, shift)
-        alone(functools.partial(piece, pairs[0], inner))
-        take(k, (0,), act)
-        alone(functools.partial(piece, pairs[1], inner))
-        for copies in rims:
-            wait_rows(copies)
-        for f in range(*pairs[0]):
-            act_outer(k, act, f, shift)
-        give(k, (1, 2), act)
-        for f in range(*pairs[1]):
-            act_outer(k, act, f, shift)
+        give(k, 1)
+        inner_rows()
+        if k == 0:
+            alone(functools.partial(piece, pairs[0], inner))
+        outer_rows()
         alone(functools.partial(piece, pairs[0], outer))
         after(0)
-        take(k, (1, 2), act)
+
+        @pl.when(later)
+        def _():
+            for part in range(3):
+                ahead(k, part).wait_recv()
+            for f in range(2):
+                mean, scale = norm_in[k, f:f + 1], norm_in[k, 2 + f:3 + f]
+                act_inner(src, act, f, mean, scale, shift)
+                act_outer(rim_prev[k, 0, f], rim_prev[k, 1, f], act, f, mean, scale, shift)
+
         alone(functools.partial(piece, pairs[1], outer))
         after(1)
+        if k == 1:
+            alone(functools.partial(piece, pairs[0], inner))
+        alone(functools.partial(piece, pairs[1], inner))
 
     def each(pair, which):
         at = 0
@@ -301,9 +316,9 @@
         wide = made.astype(f32)
         m = len(which) * cols
         for f in range(*pair):
-            add_sums(f, wide[(f - pair[0]) * m:(f - pair[0] + 1) * m], which == inner)
+            add_sums(f, wide[(f - pair[0]) * m:(f - pair[0] + 1) * m], (which == inner) == (pair == pairs[0]))
         for f, y, at in each(pair, which):
-            h_own[f, y] = made[at]
+            h_own[2 + f, y] = made[at]
             if y == rows - 1:
                 pack(1, 0, f, made[at])
             if y == 0:
@@ -312,13 +327,13 @@
     rim_h, rim_j = [], []
 
     def hidden_after(slot):
-        if slot == 1:
-            put_sums(1)
-            send_sums(1)
         rim_h.append(send_rows(1, 1 + slot, *pairs[slot]))
+        if slot == 0:
+            give(1, 0)
 
     def joined_piece(pair, which):
-        base = lines_of(x_own, pair[0], pair[1], which, 0) if which == outer else x_own[pair[0]:pair[1], 1:rows - 1]
+        f0, f1 = 2 + pair[0], 2 + pair[1]
+        base = lines_of(x_own, f0, f1, which, 0) if which == outer else x_own[f0:f1, 1:rows - 1]
         base = base.reshape(-1, chans).astype(f32)
         made = (base + (conv(act2, w2, pair, which) + vecs[5])).astype(bf16)
         wide = made.astype(f32)
@@ -333,6 +348,8 @@
         rim_j.append(send_rows(2, 3 + slot, *pairs[slot]))
 
     stage(0, x_own, act1, vecs[0], 0.5 * vecs[1], [rim_x], hidden_piece, hidden_after)
+    put_sums(1)
+    send_sums(1)
     stage(1, h_own, act2, vecs[3], 0.5 * vecs[4], rim_h, joined_piece, joined_after)
 
     def up(pair, r, y0, y1):
@@ -359,8 +376,8 @@
     for slot in range(2):
         wait_rows(rim_j[slot])
         for f in range(*pairs[slot]):
-            put_shifted(jact, f, 0, jnp.where(up_ok, unpack(2, 0, f), 0.0))
-            put_shifted(jact, f, rows + 1, jnp.where(down_ok, unpack(2, 1, f), 0.0))
+            put_shifted(jact, f, 0, jnp.where(up_ok, unpack(rim_in[2, 0, f]), 0.0))
+            put_shifted(jact, f, rows + 1, jnp.where(down_ok, unpack(rim_in[2, 1, f]), 0.0))
 
         @alone
         def _():
@@ -374,9 +391,9 @@
 
     @pl.when(first)
     def _():
-        for k, act in enumerate((act1, act2)):
+        for k in range(2):
             for part in range(3):
-                ahead(k, part, act).wait_send()
+                ahead(k, part).wait_send()
 
 
 def solution(mesh):
@@ -394,8 +411,8 @@
             in_specs=[hbm] * 11,
             out_specs=pl.BlockSpec(memory_space=pltpu.VMEM),
             scratch_shapes=[
-                pltpu.VMEM((frames, rows, cols, chans), bf16),
-                pltpu.VMEM((frames, rows, cols, chans), bf16),
+                pltpu.VMEM((frames + 2, rows, cols, chans), bf16),
+                pltpu.VMEM((frames + 2, rows, cols, chans), bf16),
                 pltpu.VMEM((frames + 2, rows + 2, cols, KP), bf16),
                 pltpu.VMEM((frames + 2, rows + 2, cols, KP), bf16),
                 pltpu.VMEM((frames, rows + 2, cols, KP), bf16),
@@ -406,12 +423,15 @@
                 pltpu.VMEM((7, 1, chans), f32),
                 pltpu.VMEM((1, chans // 2), f32),
                 pltpu.VMEM((16, chans), f32),
+                pltpu.VMEM((2, 4, chans), f32),
+                pltpu.VMEM((2, 4, chans), f32),
                 pltpu.VMEM((2 * frames, chans), f32),
                 pltpu.VMEM((chans, 128), bf16),
                 pltpu.VMEM((128, chans), bf16),
                 pltpu.VMEM((2, n, 8, 128), f32),
                 pltpu.VMEM((3, 2, frames, cols + cols // 2, 128), bf16),
                 pltpu.VMEM((3, 2, frames, cols + cols // 2, 128), bf16),
+                pltpu.VMEM((2, 2, 2, cols + cols // 2, 128), bf16),
                 pltpu.VMEM((rows + 2, cols + 16, chans), f32),
                 dma((11,)),
                 dma((5, 2)),

time: 33.5 us -> 30.5 us (0.910)
  Pallas kernels: 32.3 us -> 29.4 us
    pallas_call x1, Pallas kernels: 32.3 us -> 29.4 us  [body(): pl.pallas_call(functools.partial(kernel, n), out_shape=pltpu.VMEM((frames...]
where the time goes in v4:
time: 30.5 us; the launch traced here: 30.4 us
  Pallas kernels  29.4 us (96%)
  local copies, waits for them, and re-layouts  0.97 us (3%)
    pallas_call x1, Pallas kernels, body(): pl.pallas_call(functools.partial(kernel, n), out_shape=pltpu.VMEM((frames...  29.4 us
    unnamed x1, local copies, waits for them, and re-layouts  0.97 us

profile of v4, /device:TPU:0, one launch (start us, length us, event | category | flops | bytes accessed | tf_op | source)
XLA Modules:
  0.0 30.4 jit_solution(8238459294030111112)
XLA Ops:
  0.0 29.4 %shard_map.109 = bf16[4,8,64,192]{3,2,1,0:T(8,128)(2,1)S(1)} custom-call(bf16[4,4,64,192]{3,2,1,0:T(8,128)(2,1)} %bitcast.14, f32[1,192]{1,0:T(1,128)} %bitcast.15, f32[1,192]{1,0:T(1,128)} %bitcast.16, bf16[9,576,192]{2,1,0:T(8,128)(2,1)} %bitcast.12, f32[1,192]{1,0:T(1,128)} %bitcast.17, f32[1,192]{1,0:T(1,128)} %bitcast.18, f32[1,192]{1,0:T(1,128)} %bitcast.19, ...), custom_call_target="tpu_custom_call" | custom-call | tf_op jit(solution)/shard_map/pallas_call | solution.py:408
  29.4 1.0 %copy.13 = bf16[1,4,8,64,192]{4,3,2,1,0:T(8,128)(2,1)} copy(bf16[1,4,8,64,192]{4,3,2,1,0:T(8,128)(2,1)S(1)} %bitcast.11) | data formatting | bytes 1572864

commit v5 on v4

--- a/solution.py
+++ b/solution.py
@@ -54,8 +54,10 @@
 
     load_x = local(0, feat, x_own.at[pl.ds(2, frames)])
 
+    far = sorted(range(1, n), key=lambda d: -min(d, n - d))
+
     barrier = pltpu.get_barrier_semaphore()
-    for d in range(1, n):
+    for d in far:
         to = lax.rem(tile + d, n)
         pl.semaphore_signal(barrier, inc=1, device_id=(tm, to), device_id_type=MESH)
     pl.semaphore_signal(barrier, inc=1, device_id=(1 - tm, tile), device_id_type=MESH)
@@ -146,12 +148,13 @@
     block_of = lax.broadcasted_iota(jnp.int32, (frames, 128), 1) // G
     block = jnp.where(block_of == lax.broadcasted_iota(jnp.int32, (frames, 128), 0), 1.0, 0.0)
 
-    def put_sums(slot):
+    def put_sums(slot, f0, f1):
         @alone
         def _():
             made = split_dot(sums[...], gmap[...])
             for i in range(2):
-                stats[slot, 0, i:i + 1] = jnp.sum(made[i * frames:(i + 1) * frames] * block, axis=0, keepdims=True)
+                picked = made[i * frames + f0:i * frames + f1] * block[f0:f1]
+                stats[slot, 0, i:i + 1] = jnp.sum(picked, axis=0, keepdims=True)
 
     def add_sums(f, value, fresh):
         for i, v in enumerate((value, value * value)):
@@ -159,7 +162,7 @@
             total = jnp.sum(v, axis=0, keepdims=True)
             sums[line] = total if fresh else sums[line] + total
 
-    def norm_from(slot, gain):
+    def norm_from(k, slot, f0, f1, gain):
         @alone
         def _():
             total = jnp.sum(stats[slot, :, 0:2], axis=0)
@@ -168,15 +171,16 @@
             mean = both[0:frames]
             var = both[frames:2 * frames] - mean * mean
             scale = 0.5 * (lax.rsqrt(var + EPS) * gain)
-            norm[0:frames] = mean
-            norm[8:8 + frames] = scale
-            norm_out[slot, 0:2] = mean[old:frames]
-            norm_out[slot, 2:4] = scale[old:frames]
+            norm[f0:f1] = mean[f0:f1]
+            norm[8 + f0:8 + f1] = scale[f0:f1]
+            if f1 == frames:
+                norm_out[k, 0:2] = mean[old:frames]
+                norm_out[k, 2:4] = scale[old:frames]
 
     def put_shifted(dst, f, r, value):
-        beside[r, 8:8 + cols] = value
-        left = beside[r, 7:7 + cols]
-        right = beside[r, 9:9 + cols]
+        at = lax.broadcasted_iota(jnp.int32, (cols, 1), 0)
+        left = jnp.where(at == 0, 0.0, pltpu.roll(value, 1, 0))
+        right = jnp.where(at == cols - 1, 0.0, pltpu.roll(value, cols - 1, 0))
         dst[f, r, :, 0:chans] = left.astype(bf16)
         dst[f, r, :, chans:2 * chans] = value.astype(bf16)
         dst[f, r, :, 2 * chans:3 * chans] = right.astype(bf16)
@@ -223,7 +227,7 @@
     load_x.wait()
     for f in range(frames):
         add_sums(f, x_own[2 + f].reshape(rows * cols, chans).astype(f32), True)
-    put_sums(0)
+    put_sums(0, 0, frames)
     for f in range(frames):
         pack(0, 0, f, x_own[2 + f, rows - 1])
         pack(0, 1, f, x_own[2 + f, 0])
@@ -268,24 +272,42 @@
     load_2.wait()
 
     def stage(k, src, act, gain, shift, rims, piece, after):
-        def inner_rows():
-            for f in range(frames):
-                act_inner(src, act, 2 + f, norm[f:f + 1], norm[8 + f:9 + f], shift)
-
-        def outer_rows():
-            for copies in rims:
-                wait_rows(copies)
+        def own(f):
+            return norm[f:f + 1], norm[8 + f:9 + f], shift
+
+        def inner_rows(f0, f1):
+            for f in range(f0, f1):
+                act_inner(src, act, 2 + f, *own(f))
+
+        def outer_rows(f0, f1):
+            for f in range(f0, f1):
+                act_outer(rim_in[k, 0, f], rim_in[k, 1, f], act, 2 + f, *own(f))
+
+        def take_rims(copies):
+            for copy in copies:
+                wait_rows(copy)
             give(k, 2)
-            for f in range(frames):
-                act_outer(rim_in[k, 0, f], rim_in[k, 1, f], act, 2 + f, norm[f:f + 1], norm[8 + f:9 + f], shift)
-
-        own_all(k).wait_recv()
-        norm_from(k, gain)
-        give(k, 1)
-        inner_rows()
+
         if k == 0:
+            own_all(0).wait_recv()
+            norm_from(0, 0, 0, frames, gain)
+            give(0, 1)
+            inner_rows(0, frames)
             alone(functools.partial(piece, pairs[0], inner))
-        outer_rows()
+            take_rims(rims)
+            outer_rows(0, frames)
+        else:
+            take_rims(rims[0:1])
+            own_all(1).wait_recv()
+            norm_from(1, 1, *pairs[0], gain)
+            give(1, 1)
+            inner_rows(*pairs[0])
+            outer_rows(*pairs[0])
+            wait_rows(rims[1])
+            own_all(2).wait_recv()
+            norm_from(1, 2, *pairs[1], gain)
+            inner_rows(*pairs[1])
+            outer_rows(*pairs[1])
         alone(functools.partial(piece, pairs[0], outer))
         after(0)
 
@@ -330,6 +352,8 @@
         rim_h.append(send_rows(1, 1 + slot, *pairs[slot]))
         if slot == 0:
             give(1, 0)
+            put_sums(1, *pairs[0])
+            send_sums(1)
 
     def joined_piece(pair, which):
         f0, f1 = 2 + pair[0], 2 + pair[1]
@@ -348,8 +372,8 @@
         rim_j.append(send_rows(2, 3 + slot, *pairs[slot]))
 
     stage(0, x_own, act1, vecs[0], 0.5 * vecs[1], [rim_x], hidden_piece, hidden_after)
-    put_sums(1)
-    send_sums(1)
+    put_sums(2, *pairs[1])
+    send_sums(2)
     stage(1, h_own, act2, vecs[3], 0.5 * vecs[4], rim_h, joined_piece, joined_after)
 
     def up(pair, r, y0, y1):
@@ -428,7 +452,7 @@
                 pltpu.VMEM((2 * frames, chans), f32),
                 pltpu.VMEM((chans, 128), bf16),
                 pltpu.VMEM((128, chans), bf16),
-                pltpu.VMEM((2, n, 8, 128), f32),
+                pltpu.VMEM((3, n, 8, 128), f32),
                 pltpu.VMEM((3, 2, frames, cols + cols // 2, 128), bf16),
                 pltpu.VMEM((3, 2, frames, cols + cols // 2, 128), bf16),
                 pltpu.VMEM((2, 2, 2, cols + cols // 2, 128), bf16),
@@ -436,8 +460,8 @@
                 dma((11,)),
                 dma((5, 2)),
                 dma((5, 2)),
-                dma((2,)),
-                dma((2,)),
+                dma((3,)),
+                dma((3,)),
                 dma((2, 3)),
                 dma((2, 3)),
             ],

time: 30.5 us -> 30.1 us (0.987)
  Pallas kernels: 29.4 us -> 29 us
    pallas_call x1, Pallas kernels: 29.4 us -> 29 us  [body(): pl.pallas_call(functools.partial(kernel, n), out_shape=pltpu.VMEM((frames...]
where the time goes in v5:
time: 30.1 us; the launch traced here: 30 us
  Pallas kernels  29 us (96%)
  local copies, waits for them, and re-layouts  0.97 us (3%)
    pallas_call x1, Pallas kernels, body(): pl.pallas_call(functools.partial(kernel, n), out_shape=pltpu.VMEM((frames...  29 us
    unnamed x1, local copies, waits for them, and re-layouts  0.97 us

profile of v5, /device:TPU:0, one launch (start us, length us, event | category | flops | bytes accessed | tf_op | source)
XLA Modules:
  0.0 30.0 jit_solution(1592992115082644263)
XLA Ops:
  0.0 29.0 %shard_map.109 = bf16[4,8,64,192]{3,2,1,0:T(8,128)(2,1)S(1)} custom-call(bf16[4,4,64,192]{3,2,1,0:T(8,128)(2,1)} %bitcast.14, f32[1,192]{1,0:T(1,128)} %bitcast.15, f32[1,192]{1,0:T(1,128)} %bitcast.16, bf16[9,576,192]{2,1,0:T(8,128)(2,1)} %bitcast.12, f32[1,192]{1,0:T(1,128)} %bitcast.17, f32[1,192]{1,0:T(1,128)} %bitcast.18, f32[1,192]{1,0:T(1,128)} %bitcast.19, ...), custom_call_target="tpu_custom_call" | custom-call | tf_op jit(solution)/shard_map/pallas_call | solution.py:432
  29.0 1.0 %copy.13 = bf16[1,4,8,64,192]{4,3,2,1,0:T(8,128)(2,1)} copy(bf16[1,4,8,64,192]{4,3,2,1,0:T(8,128)(2,1)S(1)} %bitcast.11) | data formatting | bytes 1572864

commit v6 on v5

--- a/solution.py
+++ b/solution.py
@@ -69,7 +69,6 @@
     ]
     load_b = local(10, ub_h, ubv)
     load_1 = local(2, k1, w1.at[:, pl.ds(0, 3 * chans)])
-    load_2 = local(3, k2, w2.at[:, pl.ds(0, 3 * chans)])
 
     alone = pl.when(tile >= 0)
 
@@ -235,6 +234,7 @@
     send_sums(0)
     rim_x = send_rows(0, 0, 0, frames)
     give(0, 0)
+    load_2 = local(3, k2, w2.at[:, pl.ds(0, 3 * chans)])
 
     pad = KP - 3 * chans
     beside[:, 0:8] = jnp.zeros((rows + 2, 8, chans), f32)
@@ -269,7 +269,18 @@
     vecs[6, :, 0:half] = ubv[...]
     vecs[6, :, half:chans] = ubv[...]
     load_1.wait()
-    load_2.wait()
+
+    def drain(k):
+        for copy, sends, _ in pending:
+            pl.when(sends)(copy.wait_send)
+        pending.clear()
+        for slot in ((0,), (1, 2))[k]:
+            own_all(slot).wait_send()
+
+        @pl.when(first)
+        def _():
+            for part in range(3):
+                ahead(k, part).wait_send()
 
     def stage(k, src, act, gain, shift, rims, piece, after):
         def own(f):
@@ -304,6 +315,7 @@
             inner_rows(*pairs[0])
             outer_rows(*pairs[0])
             wait_rows(rims[1])
+            drain(0)
             own_all(2).wait_recv()
             norm_from(1, 2, *pairs[1], gain)
             inner_rows(*pairs[1])
@@ -374,6 +386,7 @@
     stage(0, x_own, act1, vecs[0], 0.5 * vecs[1], [rim_x], hidden_piece, hidden_after)
     put_sums(2, *pairs[1])
     send_sums(2)
+    load_2.wait()
     stage(1, h_own, act2, vecs[3], 0.5 * vecs[4], rim_h, joined_piece, joined_after)
 
     def up(pair, r, y0, y1):
@@ -408,16 +421,7 @@
             up(pairs[slot], 0, 0, 1)
             up(pairs[slot], 1, rows - 1, rows)
 
-    for copy, sends, _ in pending:
-        pl.when(sends)(copy.wait_send)
-    for slot in sent:
-        own_all(slot).wait_send()
-
-    @pl.when(first)
-    def _():
-        for k in range(2):
-            for part in range(3):
-                ahead(k, part).wait_send()
+    drain(1)
 
 
 def solution(mesh):

time: 30.1 us -> 30.1 us (level)
  no operation moved by 1% of the time
where the time goes in v6:
time: 30.1 us; the launch traced here: 30 us
  Pallas kernels  29 us (96%)
  local copies, waits for them, and re-layouts  0.97 us (3%)
    pallas_call x1, Pallas kernels, body(): pl.pallas_call(functools.partial(kernel, n), out_shape=pltpu.VMEM((frames...  29 us
    unnamed x1, local copies, waits for them, and re-layouts  0.97 us

profile of v6, /device:TPU:0, one launch (start us, length us, event | category | flops | bytes accessed | tf_op | source)
XLA Modules:
  0.0 30.0 jit_solution(5911800453772453031)
XLA Ops:
  0.0 29.0 %shard_map.109 = bf16[4,8,64,192]{3,2,1,0:T(8,128)(2,1)S(1)} custom-call(bf16[4,4,64,192]{3,2,1,0:T(8,128)(2,1)} %bitcast.14, f32[1,192]{1,0:T(1,128)} %bitcast.15, f32[1,192]{1,0:T(1,128)} %bitcast.16, bf16[9,576,192]{2,1,0:T(8,128)(2,1)} %bitcast.12, f32[1,192]{1,0:T(1,128)} %bitcast.17, f32[1,192]{1,0:T(1,128)} %bitcast.18, f32[1,192]{1,0:T(1,128)} %bitcast.19, ...), custom_call_target="tpu_custom_call" | custom-call | tf_op jit(solution)/shard_map/pallas_call | solution.py:436
  29.0 1.0 %copy.13 = bf16[1,4,8,64,192]{4,3,2,1,0:T(8,128)(2,1)} copy(bf16[1,4,8,64,192]{4,3,2,1,0:T(8,128)(2,1)S(1)} %bitcast.11) | data formatting | bytes 1572864
